TPU v7x, 32 devices: a whole 2x2x4 slice. The times are simulated.
32 devices in a mesh: groups: 2 (over x), blk: 16 (over z, y, core).
Axes of the slice: x: 2, y: 2, z: 4, core: 2. Of those that a mesh axis runs over, the one named last changes fastest.
Arguments:
- embeddings: bfloat16 [6144, 256], P(('groups', 'blk')), parts along dimension 0, may hold values from -12 to 12
- codebook: bfloat16 [16384, 256], P(('groups', 'blk')), parts along dimension 0, may hold values from -5 to 5
Outputs:
- codebook_shift: bfloat16 [16384, 256], P(('groups', 'blk')), parts along dimension 0
- occupancy: float32 [16384], P(('groups', 'blk')), parts along dimension 0
- soft_quantized: bfloat16 [6144, 256], P(('groups', 'blk')), parts along dimension 0
- row_lse: float32 [6144], P(('groups', 'blk')), parts along dimension 0
There are 2 independent parts, one for each index of `groups`. A program takes and returns all parts, laid end to end along the dimension named above; each array names one. Nothing has to cross between parts.
All inputs are finite; a program needn't handle non-finite values.
Results may differ from a plain program's by a relative error of at most 0.005.
Values may be sent and summed in bfloat16 or wider, within the bound.
No kernel may reach another device: no remote copies, remote signals or barrier semaphores. Data moves between devices by JAX's collectives and lax.ppermute only.
A program may use at most 64 MiB of HBM per device.

v0:
```python
import math
import jax
import jax.numpy as jnp
from jax import lax
from jax.sharding import PartitionSpec as P


def row_block():
    return 1024


def block_scores(rows_data, code_block, norm_term, sharpness):
    return (
        sharpness
        * jnp.einsum("rd,kd->rk", rows_data, code_block, preferred_element_type=jnp.float32)
        - norm_term[None, :]
    )


def stats_block(rows_data, code_blocks, norm_terms, sharpness):

    def stat_step(running, scanned):
        running_max, running_sum = running
        code_block, norm_term = scanned
        scores = block_scores(rows_data, code_block, norm_term, sharpness)
        new_max = jnp.maximum(running_max, jnp.max(scores, axis=1))
        running_sum = running_sum * jnp.exp(running_max - new_max) + jnp.sum(
            jnp.exp(scores - new_max[:, None]), axis=1
        )
        return ((new_max, running_sum), None)

    row_count = rows_data.shape[0]
    initial = (
        jnp.full((row_count,), -jnp.inf, dtype=jnp.float32),
        jnp.zeros((row_count,), jnp.float32),
    )
    final, ignored = lax.scan(stat_step, initial, (code_blocks, norm_terms))
    return final


def row_stats(rows_data, code_blocks, norm_terms, sharpness):
    count = rows_data.shape[0]
    size = row_block()
    blocks = rows_data.reshape(count // size, size, rows_data.shape[1])
    result = lax.map(lambda rows: stats_block(rows, code_blocks, norm_terms, sharpness), blocks)
    return (result[0].reshape(count), result[1].reshape(count))


def share_pass(rows_data, lse_rows, code_blocks, norm_terms, sharpness):
    count = rows_data.shape[0]
    width = rows_data.shape[1]
    size = row_block()
    row_blocks = rows_data.reshape(count // size, size, width)
    lse_blocks = lse_rows.reshape(count // size, size)
    block_count = code_blocks.shape[0]
    block_size = code_blocks.shape[1]
    k_dev = block_count * block_size

    def outer_step(totals, scanned):
        rows_here, lse_here = scanned

        def inner_step(rebuilt, inner):
            code_block, norm_term = inner
            scores = block_scores(rows_here, code_block, norm_term, sharpness)
            shares = jnp.exp(scores - lse_here[:, None]).astype(jnp.bfloat16)
            weighted = jnp.einsum(
                "rk,rd->kd", shares, rows_here, preferred_element_type=jnp.float32
            )
            masses = jnp.sum(shares, axis=0, dtype=jnp.float32)
            rebuilt = rebuilt + jnp.dot(shares, code_block, preferred_element_type=jnp.float32)
            return (rebuilt, (weighted, masses))

        start = jnp.zeros((size, width), jnp.float32)
        rebuilt, stacked = lax.scan(inner_step, start, (code_blocks, norm_terms))
        new_totals = (
            totals[0] + stacked[0].reshape(k_dev, width),
            totals[1] + stacked[1].reshape(k_dev),
        )
        return (new_totals, rebuilt)

    initial = (jnp.zeros((k_dev, width), jnp.float32), jnp.zeros((k_dev,), jnp.float32))
    totals, per_rows = lax.scan(outer_step, initial, (row_blocks, lse_blocks))
    return (per_rows.reshape(count, per_rows.shape[2]), totals[0], totals[1])


def on_device(embeddings, codebook):
    rows_dev = embeddings.shape[0]
    feature_width = embeddings.shape[1]
    k_dev = codebook.shape[0]
    sharpness = 3.0 / math.sqrt(feature_width)
    block_size = min(k_dev, 1024)
    block_count = k_dev // block_size
    code_blocks = codebook.reshape(block_count, block_size, feature_width)
    norm_terms = (
        0.5 * sharpness * jnp.sum(jnp.square(codebook.astype(jnp.float32)), axis=1)
    ).reshape(block_count, block_size)
    gathered = lax.all_gather(embeddings, "blk", axis=0, tiled=True)
    local_max, local_sum = row_stats(gathered, code_blocks, norm_terms, sharpness)
    global_max = lax.pmax(local_max.astype(jnp.bfloat16), "blk").astype(local_max.dtype)
    global_total = lax.psum(local_sum * jnp.exp(local_max - global_max), "blk")
    lse_all = global_max + jnp.log(global_total)
    rebuilt, weighted, masses = share_pass(gathered, lse_all, code_blocks, norm_terms, sharpness)
    own_rebuilt = lax.psum_scatter(rebuilt, "blk", scatter_dimension=0, tiled=True)
    soft_quantized = own_rebuilt.astype(jnp.bfloat16)
    prior_mass = rows_dev / k_dev
    codebook_shift = (
        (weighted - masses[:, None] * codebook.astype(jnp.float32)) / (masses[:, None] + prior_mass)
    ).astype(jnp.bfloat16)
    occupancy = masses * (k_dev / rows_dev)
    own_lse = lax.dynamic_slice_in_dim(lse_all, lax.axis_index("blk") * rows_dev, rows_dev, 0)
    return (codebook_shift, occupancy, soft_quantized, own_lse)


def solution(mesh):
    in_specs = (P(("groups", "blk"), None), P(("groups", "blk"), None))
    out_specs = (
        P(("groups", "blk"), None),
        P(("groups", "blk")),
        P(("groups", "blk"), None),
        P(("groups", "blk")),
    )
    return jax.shard_map(
        on_device, mesh=mesh, in_specs=in_specs, out_specs=out_specs, check_vma=False
    )
```

profile of v0, /device:TPU:0, one launch (start us, length us, event | category | flops | bytes accessed | tf_op | source)
XLA Modules:
  0.0 236.2 jit_solution(4751557155126825032)
XLA Ops:
  7.2 0.7 all-gather.2.cloned.1.call-update
  8.0 1.1 fusion.15
  9.1 43.6 %all-gather.2.cloned.1.call-done = bf16[3072,256]{1,0:T(8,128)(2,1)} async-done(((bf16[192,256]{1,0:T(8,128)(2,1)}), bf16[3072,256]{1,0:T(8,128)(2,1)}) %all-gather.2.cloned.1.call-update) | async-done | bytes 1572880 | tf_op jit(solution)/shard_map/all_gather | solution.py:97
  52.7 6.9 %while.27 = (s32[]{:T(128)}, f32[3,1024]{1,0:T(4,128)S(1)}, f32[3,1024]{1,0:T(4,128)S(1)}, bf16[3,1024,256]{2,1,0:T(8,128)(2,1)}, bf16[1,512,256]{2,1,0:T(8,128)...) while((s32[]{:T(128)}, f32[3,1024]{1,0:T(4,128)S(1)}, f32[3,1024]{1,0:T(4,128)S(1)}, ...), condition=%wide.region_4.5_spmd, body=%wide.region_1.4_spmd.sunk | while | flops 272106496 | bytes 5025897 | solution.py:45
  52.7 1.6 fusion.29
  54.3 0.5 exponential_reduce_fusion.2
  54.8 0.1 dynamic_update_slice.22
  54.9 0.1 dynamic_update_slice.23
  55.0 1.6 fusion.29
  56.6 0.5 exponential_reduce_fusion.2
  57.1 0.1 dynamic_update_slice.22
  57.2 0.1 dynamic_update_slice.23
  57.3 1.6 fusion.29
  58.9 0.5 exponential_reduce_fusion.2
  59.4 0.1 dynamic_update_slice.22
  59.6 32.1 %pmax.7 = bf16[3072]{0:T(1024)(128)(2,1)S(1)} all-reduce(bf16[3072]{0:T(1024)(128)(2,1)S(1)} %convert_element_type.25), channel_id=1, replica_groups=mesh['groups'=2,'blk'=16] {'blk'}, use_global_device_ids=true, to_apply=%region_5.6 | all-reduce | flops 3072 | bytes 12288 | tf_op jit(solution)/shard_map/pmax | solution.py:99
  91.7 57.6 %psum.7 = f32[3072]{0:T(1024)S(1)} all-reduce(f32[3072]{0:T(1024)S(1)} %fusion.20), channel_id=1, replica_groups=mesh['groups'=2,'blk'=16] {'blk'}, use_global_device_ids=true, to_apply=%region_6.7 | all-reduce | flops 3072 | bytes 24576 | tf_op jit(solution)/shard_map/psum | solution.py:100
  149.4 14.8 %while.28 = (s32[]{:T(128)}, f32[512,256]{1,0:T(8,128)S(1)}, f32[512]{0:T(512)S(1)}, f32[3,1024,256]{2,1,0:T(8,128)}, bf16[3,1024,256]{2,1,0:T(8,128)(2,1)}, /*i...) while((s32[]{:T(128)}, f32[512,256]{1,0:T(8,128)S(1)}, ...), condition=%wide.region_9.10_spmd.clone, body=%wide.region_7.9_spmd.clone.sunk | while | flops 808714752 | bytes 7887012 | solution.py:82
  149.4 1.8 convert_reduce_fusion.2
  151.2 1.7 convolution_add_fusion.2
  152.9 1.4 fusion.34
  154.3 1.8 convert_reduce_fusion.2
  156.1 1.7 convolution_add_fusion.2
  157.8 1.5 fusion.34
  159.3 1.8 convert_reduce_fusion.2
  161.1 1.7 convolution_add_fusion.2
  162.8 1.4 fusion.34
  164.2 0.6 dynamic_slice.24
  164.9 0.6 broadcast_multiply_fusion
  165.4 0.9 fusion.18
  166.4 61.4 %reduce-scatter.2.cloned.1.call-done = f32[192,256]{1,0:T(8,128)} async-done(((f32[3072,256]{1,0:T(8,128)}), f32[192,256]{1,0:T(8,128)}) %reduce-scatter.2.cloned.1.call-update) | async-done | bytes 196624 | tf_op jit(solution)/shard_map/reduce_scatter | solution.py:103
  227.8 1.6 convert_element_type.28
  (33 shorter events, 0.4 us)
Async XLA Ops:
  7.2 45.5 %all-gather.2.cloned.1.call-start = ((), (), s32[]{:S(2)}) async-start(), calls=%async_computation.1 | async-start | bytes 1671168 | tf_op jit(solution)/shard_map/all_gather | solution.py:97
  7.9 219.9 %reduce-scatter.2.cloned.1.call-start = ((), (), s32[]{:S(2)}) async-start(), calls=%async_computation.2 | async-start | bytes 3342336 | tf_op jit(solution)/shard_map/reduce_scatter | solution.py:103
  151.2 1.7 copy-start
  156.1 1.7 copy-start
  161.1 1.7 copy-start
  164.2 1.3 copy-start.1
Sparse Core Ops, SparseCore 0:
  10.3 42.3 all-gather.1
  164.3 63.4 reduce-scatter.1
where the time goes:
time: 237 us; the launch traced here: 236 us
  waiting for transfers between devices  106 us (45%)
  blocking collectives  89.7 us (38%)
  matrix products  19.4 us (8%)
  between operations  14.1 us (6%)
  other arithmetic  5.73 us (2%)
    reduce_scatter x1, waiting for transfers between devices, on_device(): lax.psum_scatter(rebuilt, 'blk', scatter_dimension=0, tiled=True)  61.4 us
    psum x1, blocking collectives, on_device(): global_total = lax.psum(local_sum * jnp.exp(local_max - global_max), 'blk')  57.6 us
    all_gather x1, waiting for transfers between devices, on_device(): gathered = lax.all_gather(embeddings, 'blk', axis=0, tiled=True)  43.6 us
    pmax x1, blocking collectives, on_device(): lax.pmax(local_max.astype(jnp.bfloat16), 'blk').astype(local_max.dtype)  32.1 us
    dot_general x6, matrix products, block_scores(): jnp.einsum('rd,kd->rk', rows_data, code_block, preferred_element_type=jnp...  10.1 us
    dot_general x3, matrix products, inner_step(): jnp.einsum('rk,rd->kd', shares, rows_here, preferred_element_type=jnp.flo...  4.99 us
  transfers between devices with their start and end apart: 2, of which 2 were waited for; matrix products, arithmetic and copies ran while one was open for 1% of the time, Pallas kernels for 0%

commit v1 on v0

--- a/solution.py
+++ b/solution.py
@@ -97,7 +97,9 @@
     gathered = lax.all_gather(embeddings, "blk", axis=0, tiled=True)
     local_max, local_sum = row_stats(gathered, code_blocks, norm_terms, sharpness)
     global_max = lax.pmax(local_max.astype(jnp.bfloat16), "blk").astype(local_max.dtype)
-    global_total = lax.psum(local_sum * jnp.exp(local_max - global_max), "blk")
+    global_total = jnp.sum(
+        lax.all_gather(local_sum * jnp.exp(local_max - global_max), "blk"), axis=0
+    )
     lse_all = global_max + jnp.log(global_total)
     rebuilt, weighted, masses = share_pass(gathered, lse_all, code_blocks, norm_terms, sharpness)
     own_rebuilt = lax.psum_scatter(rebuilt, "blk", scatter_dimension=0, tiled=True)

time: 237 us -> 198 us (0.84)
  blocking collectives: 89.7 us -> 49.8 us
    psum x1 -> x0, blocking collectives: 57.6 us -> none  [on_device(): global_total = lax.psum(local_sum * jnp.exp(local_max - global_max), 'blk')]
    all_gather x0 -> x1, blocking collectives: none -> 17.7 us  [on_device(): lax.all_gather(local_sum * jnp.exp(local_max - global_max), 'blk')]
  transfers between devices with their start and end apart: 2 -> 2, of which waited for: 2 -> 2; matrix products, arithmetic and copies ran while one was open for 1% -> 2% of each run, Pallas kernels for 0% -> 0%
where the time goes in v1:
time: 198 us
  waiting for transfers between devices  107 us (54%)
  blocking collectives  49.8 us (25%)
  matrix products  19.4 us (10%)
  between operations  14.2 us (7%)
  other arithmetic  5.77 us (3%)
    reduce_scatter x1, waiting for transfers between devices, on_device(): lax.psum_scatter(rebuilt, 'blk', scatter_dimension=0, tiled=True)  63 us
    all_gather x1, waiting for transfers between devices, on_device(): gathered = lax.all_gather(embeddings, 'blk', axis=0, tiled=True)  43.6 us
    pmax x1, blocking collectives, on_device(): lax.pmax(local_max.astype(jnp.bfloat16), 'blk').astype(local_max.dtype)  32.1 us
    all_gather x1, blocking collectives, on_device(): lax.all_gather(local_sum * jnp.exp(local_max - global_max), 'blk')  17.7 us
    dot_general x6, matrix products, block_scores(): jnp.einsum('rd,kd->rk', rows_data, code_block, preferred_element_type=jnp...  10.1 us
    dot_general x3, matrix products, inner_step(): jnp.einsum('rk,rd->kd', shares, rows_here, preferred_element_type=jnp.flo...  4.98 us
    dot_general x3, matrix products, inner_step(): jnp.dot(shares, code_block, preferred_element_type=jnp.float32)  4.33 us
  transfers between devices with their start and end apart: 2, of which 2 were waited for; matrix products, arithmetic and copies ran while one was open for 2% of the time, Pallas kernels for 0%

profile of v1, /device:TPU:0, one launch (start us, length us, event | category | flops | bytes accessed | tf_op | source)
XLA Modules:
  0.0 198.0 jit_solution(12839269115954113677)
XLA Ops:
  7.2 0.7 all-gather.3.cloned.1.call-update
  8.0 1.1 fusion.15
  9.1 43.6 %all-gather.3.cloned.1.call-done = bf16[3072,256]{1,0:T(8,128)(2,1)} async-done(((bf16[192,256]{1,0:T(8,128)(2,1)}), bf16[3072,256]{1,0:T(8,128)(2,1)}) %all-gather.3.cloned.1.call-update) | async-done | bytes 1572880 | tf_op jit(solution)/shard_map/all_gather | solution.py:97
  52.7 6.9 %while.27 = (s32[]{:T(128)}, f32[3,1024]{1,0:T(4,128)S(1)}, f32[3,1024]{1,0:T(4,128)S(1)}, bf16[3,1024,256]{2,1,0:T(8,128)(2,1)}, bf16[1,512,256]{2,1,0:T(8,128)...) while((s32[]{:T(128)}, f32[3,1024]{1,0:T(4,128)S(1)}, f32[3,1024]{1,0:T(4,128)S(1)}, ...), condition=%wide.region_4.5_spmd, body=%wide.region_1.4_spmd.sunk | while | flops 272106496 | bytes 5025897 | solution.py:45
  52.7 1.6 fusion.29
  54.3 0.5 exponential_reduce_fusion.2
  54.8 0.1 dynamic_update_slice.22
  54.9 0.1 dynamic_update_slice.23
  55.0 1.6 fusion.29
  56.6 0.5 exponential_reduce_fusion.2
  57.1 0.1 dynamic_update_slice.22
  57.2 0.1 dynamic_update_slice.23
  57.3 1.6 fusion.29
  58.9 0.5 exponential_reduce_fusion.2
  59.4 0.1 dynamic_update_slice.22
  59.6 32.1 %pmax.7 = bf16[3072]{0:T(1024)(128)(2,1)S(1)} all-reduce(bf16[3072]{0:T(1024)(128)(2,1)S(1)} %convert_element_type.25), channel_id=1, replica_groups=mesh['groups'=2,'blk'=16] {'blk'}, use_global_device_ids=true, to_apply=%region_5.6 | all-reduce | flops 3072 | bytes 12288 | tf_op jit(solution)/shard_map/pmax | solution.py:99
  91.7 17.7 %all-gather = f32[49152]{0:T(1024)S(1)} all-gather(f32[3072]{0:T(1024)S(1)} %fusion.20), channel_id=2, replica_groups=mesh['groups'=2,'blk'=16] {'blk'}, dimensions={0}, use_global_device_ids=true | all-gather | bytes 208896 | tf_op jit(solution)/shard_map/all_gather | solution.py:101
  109.5 14.8 %while.28 = (s32[]{:T(128)}, f32[512,256]{1,0:T(8,128)S(1)}, f32[512]{0:T(512)S(1)}, f32[3,1024,256]{2,1,0:T(8,128)}, bf16[3,1024,256]{2,1,0:T(8,128)(2,1)}, /*i...) while((s32[]{:T(128)}, f32[512,256]{1,0:T(8,128)S(1)}, ...), condition=%wide.region_9.10_spmd.clone, body=%wide.region_7.9_spmd.clone.sunk | while | flops 808714752 | bytes 7887012 | solution.py:82
  109.6 1.8 convert_reduce_fusion.2
  111.4 1.7 convolution_add_fusion.2
  113.0 1.4 fusion.34
  114.5 1.8 convert_reduce_fusion.2
  116.3 1.7 convolution_add_fusion.2
  118.0 1.5 fusion.34
  119.4 1.8 convert_reduce_fusion.2
  121.2 1.7 convolution_add_fusion.2
  122.9 1.4 fusion.34
  124.4 0.6 dynamic_slice.24
  125.0 0.6 broadcast_multiply_fusion
  125.6 0.9 fusion.18
  126.5 63.0 %reduce-scatter.2.cloned.1.call-done = f32[192,256]{1,0:T(8,128)} async-done(((f32[3072,256]{1,0:T(8,128)}), f32[192,256]{1,0:T(8,128)}) %reduce-scatter.2.cloned.1.call-update) | async-done | bytes 196624 | tf_op jit(solution)/shard_map/reduce_scatter | solution.py:105
  189.5 1.6 convert_element_type.28
  (35 shorter events, 0.4 us)
Async XLA Ops:
  7.2 45.5 %all-gather.3.cloned.1.call-start = ((), (), s32[]{:S(2)}) async-start(), calls=%async_computation.1 | async-start | bytes 1671168 | tf_op jit(solution)/shard_map/all_gather | solution.py:97
  7.9 181.6 %reduce-scatter.2.cloned.1.call-start = ((), (), s32[]{:S(2)}) async-start(), calls=%async_computation.2 | async-start | bytes 3342336 | tf_op jit(solution)/shard_map/reduce_scatter | solution.py:105
  111.3 1.7 copy-start
  116.2 1.7 copy-start
  121.2 1.7 copy-start
  124.3 1.3 copy-start.1
Sparse Core Ops, SparseCore 0:
  10.3 42.3 all-gather.2
  124.5 65.0 reduce-scatter.1
